TPU v7x, 256 devices: a whole 4x4x8 slice. The times are simulated.
256 devices in a mesh: row: 8 (over x, core), col: 32 (over z, y).
Axes of the slice: x: 4, y: 4, z: 8, core: 2. Of those that a mesh axis runs over, the one named last changes fastest.
Arguments:
- blocks: bfloat16 [12288, 27, 48, 48], P(('row', 'col')), may hold values from -0.59765625 to 0.59765625
- prolong: bfloat16 [12288, 48, 48], P(('row', 'col')), may hold values from -0.875 to 0.875
- columns: int32 [12288, 27], P(('row', 'col')), may hold values from 0 to 383
- aggregate: int32 [12288], P(('row', 'col')), may hold values from 0 to 15
- slots: int32 [12288, 27], P(('row', 'col')), may hold values from 0 to 26
Outputs:
- coarse: float32 [128, 27, 2304], P('row', None, 'col')
Inputs may be any that keep to these rules, and one draw needn't show every extreme that they name: `columns`: a fine block row's neighbours all lie in its column tile: the fine block rows of the devices with the same col index, in order of their row index.
All inputs are finite; a program needn't handle non-finite values.
Results may differ from a plain program's by a relative error of at most 0.0029.
Values may be sent and summed in bfloat16 or wider, within the bound.
No kernel may reach another device: no remote copies, remote signals or barrier semaphores. Data moves between devices by JAX's collectives and lax.ppermute only.
A program may use at most 192 MiB of HBM per device.

v0:
```python
import jax
import jax.numpy as jnp
from jax import lax
from jax.sharding import PartitionSpec as P

KC = 27
CR_SLAB = 16


def shards(blocks, prolong, columns, aggregate, slots):
    width = blocks.shape[2]
    tile = lax.all_gather(prolong, "row", axis=0, tiled=True)
    picked = jnp.take(tile, columns, axis=0)
    product = jnp.einsum(
        "rkab,rkbc->rkac", blocks, picked, preferred_element_type=jnp.float32
    ).astype(jnp.bfloat16)
    term = jnp.einsum("rba,rkbc->rkac", prolong, product, preferred_element_type=jnp.float32)
    target = (aggregate[:, None] * KC + slots).reshape(-1)
    partial_value = jax.ops.segment_sum(
        term.reshape(-1, width * width), target, num_segments=CR_SLAB * KC
    )
    partial_value = partial_value.reshape(CR_SLAB, KC, width * width)
    summed = lax.psum(partial_value, "col")
    share = width * width // lax.axis_size("col")
    result = lax.dynamic_slice_in_dim(summed, lax.axis_index("col") * share, share, 2)
    return result


def solution(mesh):
    return jax.shard_map(
        shards,
        mesh=mesh,
        in_specs=(
            P(("row", "col"), None, None, None),
            P(("row", "col"), None, None),
            P(("row", "col"), None),
            P(("row", "col")),
            P(("row", "col"), None),
        ),
        out_specs=P("row", None, "col"),
        check_vma=False,
    )
```

profile of v0, /device:TPU:2, one launch (start us, length us, event | category | flops | bytes accessed | tf_op | source)
XLA Modules:
  0.0 371.9 jit_solution(16122000803956569116)
XLA Ops:
  6.5 0.0 all-gather.2.cloned.1.call-start
  6.5 0.7 all-gather.2.cloned.1.call-update
  7.3 0.0 all-reduce.2.cloned.1.call-start
  7.3 0.7 compare_select_fusion
  8.0 0.1 copy.14
  8.1 0.1 reshape.17
  8.2 0.7 compare_and_fusion
  9.0 0.1 copy.13
  9.1 0.7 broadcast_multiply_fusion
  9.7 0.7 broadcast_add_fusion
  10.4 0.1 copy.12
  10.5 0.1 reshape.25
  10.7 37.4 %all-gather.2.cloned.1.call-done = bf16[384,48,48]{2,1,0:T(8,128)(2,1)} async-done(((bf16[48,48,48]{2,1,0:T(8,128)(2,1)}), bf16[384,48,48]{2,1,0:T(8,128)(2,1)}) %all-gather.2.cloned.1.call-update) | async-done | bytes 1769488 | tf_op jit(solution)/shard_map/all_gather | solution.py:12
  48.0 10.4 %gather_fusion = bf16[1296,48,48]{2,1,0:T(8,128)(2,1)} fusion(bf16[384,48,48]{2,1,0:T(8,128)(2,1)} %all-gather.2.cloned.1.call-done, s32[2048]{0:T(1024)S(1)} %pad_clamp_fusion), kind=kCustom, calls=%fused_computation | custom fusion | bytes 11949120 | tf_op jit(solution)/shard_map/jit(_take)/gather | solution.py:13
  58.5 0.0 copy-start
  58.5 22.0 %copy.15 = bf16[48,27,48,48]{2,3,1,0:T(8,128)(2,1)} copy(bf16[48,27,48,48]{3,2,1,0:T(8,128)(2,1)} %bitcast.16) | data formatting | bytes 11943936 | tf_op jit(solution)/shard_map/jit(_take)/gather | solution.py:13
  80.4 0.0 copy-done
  80.4 27.9 %fusion.10 = f32[48,27,48,48]{2,3,1,0:T(8,128)} fusion(bf16[48,27,48,48]{3,2,1,0:T(8,128)(2,1)} %param.5, bf16[48,27,48,48]{2,3,1,0:T(8,128)(2,1)} %copy.15, pred[48,27]{1,0:T(8,128)(4,1)S(1)} %copy.13, bf16[48,48,48]{2,1,0:T(8,128)(2,1)S(1)} %copy-done), kind=kOutput, calls=%fused_computation.8 | convolution fusion | flops 579280896 | bytes 24110352 | tf_op jit(solution)/shard_map/rba,rkbc->rkac/dot_general | solution.py:17
  108.3 32.6 %copy.16 = f32[48,27,48,48]{3,2,1,0:T(8,128)} copy(f32[48,27,48,48]{2,3,1,0:T(8,128)} %fusion.10) | data formatting | bytes 23887872 | tf_op jit(solution)/shard_map/rba,rkbc->rkac/transpose | solution.py:17
  140.9 25.7 %reshape.27 = f32[1296,2304]{1,0:T(8,128)} reshape(f32[48,27,48,48]{3,2,1,0:T(8,128)} %copy.16) | data formatting | bytes 23887872 | tf_op jit(solution)/shard_map/reshape | solution.py:20
  166.6 24.2 %scatter_custom_fusion = f32[432,2304]{1,0:T(8,128)} fusion(s32[1296]{0:T(1024)S(1)} %reshape.25, f32[1296,2304]{1,0:T(8,128)} %reshape.27, f32[]{:T(128)} %constant.9.clone.1), kind=kCustom, calls=%fused_computation.10 | custom fusion | flops 2985984 | bytes 3981824 | tf_op jit(solution)/shard_map/scatter-add | solution.py:19
  190.8 3.9 %reshape.14 = f32[16,27,2304]{2,1,0:T(8,128)} reshape(f32[432,2304]{1,0:T(8,128)} %scatter_custom_fusion) | data formatting | bytes 7962624 | tf_op jit(solution)/shard_map/reshape | solution.py:22
  194.7 0.0 all-reduce.2.cloned.1.call-update
  194.8 168.3 %all-reduce.2.cloned.1.call-done = f32[16,27,2304]{2,1,0:T(8,128)} async-done(((f32[16,27,2304]{2,1,0:T(8,128)}), f32[16,27,2304]{2,1,0:T(8,128)}) %all-reduce.2.cloned.1.call-update) | async-done | bytes 3981328 | tf_op jit(solution)/shard_map/psum | solution.py:23
  363.1 1.2 constant_dynamic-slice_fusion
  364.3 0.8 copy.17
  (1 shorter events, 0.0 us)
Async XLA Ops:
  6.5 41.5 %all-gather.2.cloned.1.call-start = ((), (), s32[]{:S(2)}) async-start(), calls=%async_computation | async-start | bytes 5308416 | tf_op jit(solution)/shard_map/all_gather | solution.py:12
  7.3 355.8 %all-reduce.2.cloned.1.call-start = ((), (), s32[]{:S(2)}) async-start(), calls=%async_computation.1 | async-start | bytes 9437184 | tf_op jit(solution)/shard_map/psum | solution.py:23
  58.5 22.0 %copy-start = (bf16[48,48,48]{2,1,0:T(8,128)(2,1)S(1)}, bf16[48,48,48]{2,1,0:T(8,128)(2,1)}, u32[]{:S(2)}) copy-start(bf16[48,48,48]{2,1,0:T(8,128)(2,1)} %param.6) | copy-start | bytes 663556
Sparse Core Ops, SparseCore 0:
  9.2 38.8 all-gather.1
  194.9 168.1 all-reduce.1
where the time goes:
time: 374 us; the launch traced here: 372 us
  waiting for transfers between devices  206 us (55%)
  local copies, waits for them, and re-layouts  97.1 us (26%)
  matrix products  27.9 us (7%)
  other arithmetic  27.1 us (7%)
  between operations  13.4 us (4%)
    psum x1, waiting for transfers between devices, shards(): summed = lax.psum(partial_value, 'col')  168 us
    all_gather x1, waiting for transfers between devices, shards(): tile = lax.all_gather(prolong, 'row', axis=0, tiled=True)  37.4 us
    transpose x1, local copies, waits for them, and re-layouts, shards(): jnp.einsum('rba,rkbc->rkac', prolong, product, preferred_element_type=jnp...  32.6 us
    gather x2, local copies, waits for them, and re-layouts, shards(): picked = jnp.take(tile, columns, axis=0)  32.4 us
    dot_general x1, matrix products, shards(): jnp.einsum('rba,rkbc->rkac', prolong, product, preferred_element_type=jnp...  27.9 us
    reshape x1, local copies, waits for them, and re-layouts, shards(): term.reshape(-1, width * width)  25.7 us
    scatter-add x1, other arithmetic, shards(): jax.ops.segment_sum(term.reshape(-1, width * width), target, num_segments...  24.2 us
  transfers between devices with their start and end apart: 2, of which 2 were waited for; matrix products, arithmetic and copies ran while one was open for 1% of the time, Pallas kernels for 0%

commit v1 on v0

--- a/solution.py
+++ b/solution.py
@@ -20,7 +20,10 @@
         term.reshape(-1, width * width), target, num_segments=CR_SLAB * KC
     )
     partial_value = partial_value.reshape(CR_SLAB, KC, width * width)
-    summed = lax.psum(partial_value, "col")
+    n_dev, summed = (lax.axis_size("col"), partial_value)
+    for stride in [1 << k for k in range(n_dev.bit_length() - 1)]:
+        swap = [(i, i ^ stride) for i in range(n_dev)]
+        summed = summed + lax.ppermute(summed, "col", swap)
     share = width * width // lax.axis_size("col")
     result = lax.dynamic_slice_in_dim(summed, lax.axis_index("col") * share, share, 2)
     return result

time: 374 us -> 834 us (2.23)
  waiting for transfers between devices: 206 us -> 637 us
  starting transfers between devices: 0.04 us -> 14.9 us
  other arithmetic: 27.1 us -> 37.3 us
    ppermute x0 -> x5, waiting for transfers between devices: none -> 599 us  [shards(): summed = summed + lax.ppermute(summed, 'col', swap)]
    psum x1 -> x0, waiting for transfers between devices: 168 us -> none  [shards(): summed = lax.psum(partial_value, 'col')]
    ppermute x0 -> x5, starting transfers between devices: none -> 14.9 us  [shards(): summed = summed + lax.ppermute(summed, 'col', swap)]
    add x0 -> x5, other arithmetic: none -> 10.3 us  [shards(): summed = summed + lax.ppermute(summed, 'col', swap)]
  transfers between devices with their start and end apart: 2 -> 6, of which waited for: 2 -> 6; matrix products, arithmetic and copies ran while one was open for 1% -> 0% of each run, Pallas kernels for 0% -> 0%
where the time goes in v1:
time: 834 us; the launch traced here: 830 us
  waiting for transfers between devices  637 us (76%)
  local copies, waits for them, and re-layouts  99.7 us (12%)
  other arithmetic  37.3 us (4%)
  matrix products  27.9 us (3%)
  starting transfers between devices  14.9 us (2%)
  between operations  13.4 us (2%)
    ppermute x5, waiting for transfers between devices, shards(): summed = summed + lax.ppermute(summed, 'col', swap)  599 us
    all_gather x1, waiting for transfers between devices, shards(): tile = lax.all_gather(prolong, 'row', axis=0, tiled=True)  37.4 us
    transpose x1, local copies, waits for them, and re-layouts, shards(): jnp.einsum('rba,rkbc->rkac', prolong, product, preferred_element_type=jnp...  32.6 us
    gather x2, local copies, waits for them, and re-layouts, shards(): picked = jnp.take(tile, columns, axis=0)  32.4 us
    dot_general x1, matrix products, shards(): jnp.einsum('rba,rkbc->rkac', prolong, product, preferred_element_type=jnp...  27.9 us
    reshape x1, local copies, waits for them, and re-layouts, shards(): term.reshape(-1, width * width)  25.7 us
    scatter-add x1, other arithmetic, shards(): jax.ops.segment_sum(term.reshape(-1, width * width), target, num_segments...  24.2 us
  transfers between devices with their start and end apart: 6, of which 6 were waited for; matrix products, arithmetic and copies ran while one was open for 0% of the time, Pallas kernels for 0%

profile of v1, /device:TPU:2, one launch (start us, length us, event | category | flops | bytes accessed | tf_op | source)
XLA Modules:
  0.0 830.5 jit_solution(6747766278406838693)
XLA Ops:
  6.5 0.0 all-gather.2.cloned.1.call-start
  6.5 0.7 all-gather.2.cloned.1.call-update
  7.3 0.7 compare_select_fusion
  8.0 0.1 copy.30
  8.1 0.1 reshape.17
  8.2 0.7 compare_and_fusion
  8.9 0.1 copy.29
  9.0 0.7 broadcast_multiply_fusion
  9.7 0.7 broadcast_add_fusion
  10.4 0.1 copy.28
  10.5 0.1 reshape.25
  10.6 37.4 %all-gather.2.cloned.1.call-done = bf16[384,48,48]{2,1,0:T(8,128)(2,1)} async-done(((bf16[48,48,48]{2,1,0:T(8,128)(2,1)}), bf16[384,48,48]{2,1,0:T(8,128)(2,1)}) %all-gather.2.cloned.1.call-update) | async-done | bytes 1769488 | tf_op jit(solution)/shard_map/all_gather | solution.py:12
  48.0 10.4 %gather_fusion = bf16[1296,48,48]{2,1,0:T(8,128)(2,1)} fusion(bf16[384,48,48]{2,1,0:T(8,128)(2,1)} %all-gather.2.cloned.1.call-done, s32[2048]{0:T(1024)S(1)} %pad_clamp_fusion), kind=kCustom, calls=%fused_computation | custom fusion | bytes 11949120 | tf_op jit(solution)/shard_map/jit(_take)/gather | solution.py:13
  58.5 0.0 copy-start
  58.5 21.9 %copy.31 = bf16[48,27,48,48]{2,3,1,0:T(8,128)(2,1)} copy(bf16[48,27,48,48]{3,2,1,0:T(8,128)(2,1)} %bitcast.16) | data formatting | bytes 11943936 | tf_op jit(solution)/shard_map/jit(_take)/gather | solution.py:13
  80.4 0.0 copy-done
  80.4 27.9 %fusion.10 = f32[48,27,48,48]{2,3,1,0:T(8,128)} fusion(bf16[48,27,48,48]{3,2,1,0:T(8,128)(2,1)} %param.5, bf16[48,27,48,48]{2,3,1,0:T(8,128)(2,1)} %copy.31, pred[48,27]{1,0:T(8,128)(4,1)S(1)} %copy.29, bf16[48,48,48]{2,1,0:T(8,128)(2,1)S(1)} %copy-done), kind=kOutput, calls=%fused_computation.8 | convolution fusion | flops 579280896 | bytes 24110352 | tf_op jit(solution)/shard_map/rba,rkbc->rkac/dot_general | solution.py:17
  108.3 32.6 %copy.32 = f32[48,27,48,48]{3,2,1,0:T(8,128)} copy(f32[48,27,48,48]{2,3,1,0:T(8,128)} %fusion.10) | data formatting | bytes 23887872 | tf_op jit(solution)/shard_map/rba,rkbc->rkac/transpose | solution.py:17
  140.9 25.7 %reshape.27 = f32[1296,2304]{1,0:T(8,128)} reshape(f32[48,27,48,48]{3,2,1,0:T(8,128)} %copy.32) | data formatting | bytes 23887872 | tf_op jit(solution)/shard_map/reshape | solution.py:20
  166.5 24.2 %scatter_custom_fusion = f32[432,2304]{1,0:T(8,128)} fusion(s32[1296]{0:T(1024)S(1)} %reshape.25, f32[1296,2304]{1,0:T(8,128)} %reshape.27, f32[]{:T(128)} %constant.9.clone.1), kind=kCustom, calls=%fused_computation.10 | custom fusion | flops 2985984 | bytes 3981824 | tf_op jit(solution)/shard_map/scatter-add | solution.py:19
  190.8 3.9 reshape.14
  194.7 4.6 copy.34
  199.4 1.8 collective-permute-start
  201.1 86.7 %collective-permute-done = f32[16,27,2304]{2,0,1:T(8,128)S(1)} collective-permute-done((f32[16,27,2304]{2,0,1:T(8,128)S(1)}, f32[16,27,2304]{2,0,1:T(8,128)S(1)}, u32[]{:S(2)}, u32[]{:S(2)}) %collective-permute-start) | collective-permute-done | bytes 3981344 | tf_op jit(solution)/shard_map/ppermute | solution.py:26
  287.8 5.1 copy_add_fusion
  292.9 3.1 collective-permute-start.1
  296.0 85.8 %collective-permute-done.1 = f32[16,27,2304]{2,0,1:T(8,128)S(1)} collective-permute-done((f32[16,27,2304]{2,0,1:T(8,128)S(1)}, f32[16,27,2304]{2,0,1:T(8,128)S(1)}, u32[]{:S(2)}, u32[]{:S(2)}) %collective-permute-start.1) | collective-permute-done | bytes 3981344 | tf_op jit(solution)/shard_map/ppermute | solution.py:26
  381.9 0.4 add.41
  382.3 1.6 collective-permute-start.2
  383.9 84.9 %collective-permute-done.2 = f32[16,27,2304]{2,0,1:T(8,128)S(1)} collective-permute-done((f32[16,27,2304]{2,0,1:T(8,128)S(1)}, f32[16,27,2304]{2,0,1:T(8,128)S(1)}, u32[]{:S(2)}, u32[]{:S(2)}) %collective-permute-start.2) | collective-permute-done | bytes 3981344 | tf_op jit(solution)/shard_map/ppermute | solution.py:26
  468.8 0.4 add.42
  469.2 2.6 collective-permute-start.3
  471.8 169.2 %collective-permute-done.3 = f32[16,27,2304]{2,0,1:T(8,128)S(1)} collective-permute-done((f32[16,27,2304]{2,0,1:T(8,128)S(1)}, f32[16,27,2304]{2,0,1:T(8,128)S(1)}, u32[]{:S(2)}, u32[]{:S(2)}) %collective-permute-start.3) | collective-permute-done | bytes 3981344 | tf_op jit(solution)/shard_map/ppermute | solution.py:26
  641.0 2.3 add.43
  643.3 5.7 collective-permute-start.4
  649.0 172.6 %collective-permute-done.4 = f32[16,27,2304]{2,0,1:T(8,128)} collective-permute-done((f32[16,27,2304]{2,0,1:T(8,128)}, f32[16,27,2304]{2,0,1:T(8,128)}, u32[]{:S(2)}, u32[]{:S(2)}) %collective-permute-start.4) | collective-permute-done | bytes 3981344 | tf_op jit(solution)/shard_map/ppermute | solution.py:26
  821.6 2.0 dynamic-slice_add_fusion
  (1 shorter events, 0.0 us)
Async XLA Ops:
  6.5 41.5 %all-gather.2.cloned.1.call-start = ((), (), s32[]{:S(2)}) async-start(), calls=%async_computation | async-start | bytes 5308416 | tf_op jit(solution)/shard_map/all_gather | solution.py:12
  58.5 21.9 %copy-start = (bf16[48,48,48]{2,1,0:T(8,128)(2,1)S(1)}, bf16[48,48,48]{2,1,0:T(8,128)(2,1)}, u32[]{:S(2)}) copy-start(bf16[48,48,48]{2,1,0:T(8,128)(2,1)} %param.6) | copy-start | bytes 663556
  199.4 88.5 %collective-permute-start = (f32[16,27,2304]{2,0,1:T(8,128)S(1)}, f32[16,27,2304]{2,0,1:T(8,128)S(1)}, u32[]{:S(2)}, u32[]{:S(2)}) collective-permute-start(f32[16,27,2304]{2,0,1:T(8,128)S(1)} %copy.34), channel_id=1, source_target_pairs={{0,1},{1,0},{2,3},{3,2},{4,5},{5,4},{6,7},{7,6},{8,9},{9,8},{10,11... | collective-permute-start | bytes 11943944 | tf_op jit(solution)/shard_map/ppermute | solution.py:26
  292.9 88.9 %collective-permute-start.1 = (f32[16,27,2304]{2,0,1:T(8,128)S(1)}, f32[16,27,2304]{2,0,1:T(8,128)S(1)}, u32[]{:S(2)}, u32[]{:S(2)}) collective-permute-start(f32[16,27,2304]{2,0,1:T(8,128)S(1)} %copy_add_fusion), channel_id=1, source_target_pairs={{0,2},{1,3},{2,0},{3,1},{4,6},{5,7},{6,4},{7,5},{8,10},{9,11},{10,... | collective-permute-start | bytes 11943944 | tf_op jit(solution)/shard_map/ppermute | solution.py:26
  382.3 86.5 %collective-permute-start.2 = (f32[16,27,2304]{2,0,1:T(8,128)S(1)}, f32[16,27,2304]{2,0,1:T(8,128)S(1)}, u32[]{:S(2)}, u32[]{:S(2)}) collective-permute-start(f32[16,27,2304]{2,0,1:T(8,128)S(1)} %add.41), channel_id=1, source_target_pairs={{0,4},{1,5},{2,6},{3,7},{4,0},{5,1},{6,2},{7,3},{8,12},{9,13},{10,... | collective-permute-start | bytes 11943944 | tf_op jit(solution)/shard_map/ppermute | solution.py:26
  469.2 171.8 %collective-permute-start.3 = (f32[16,27,2304]{2,0,1:T(8,128)S(1)}, f32[16,27,2304]{2,0,1:T(8,128)S(1)}, u32[]{:S(2)}, u32[]{:S(2)}) collective-permute-start(f32[16,27,2304]{2,0,1:T(8,128)S(1)} %add.42), channel_id=1, source_target_pairs={{0,8},{1,9},{2,10},{3,11},{4,12},{5,13},{6,14},{7,15},{8,0},{9,1},... | collective-permute-start | bytes 11943944 | tf_op jit(solution)/shard_map/ppermute | solution.py:26
  643.3 178.3 %collective-permute-start.4 = (f32[16,27,2304]{2,0,1:T(8,128)}, f32[16,27,2304]{2,0,1:T(8,128)}, u32[]{:S(2)}, u32[]{:S(2)}) collective-permute-start(f32[16,27,2304]{2,0,1:T(8,128)} %add.43), channel_id=1, source_target_pairs={{0,16},{1,17},{2,18},{3,19},{4,20},{5,21},{6,22},{7,23},{8,24},{9,... | collective-permute-start | bytes 11943944 | tf_op jit(solution)/shard_map/ppermute | solution.py:26
Sparse Core Ops, SparseCore 0:
  9.2 38.8 all-gather.1
